TPU v7x, 32 devices: a whole 2x2x4 slice. The times are simulated.
32 devices in a mesh: rec: 4 (over y, core), tm: 8 (over z, x).
Axes of the slice: x: 2, y: 2, z: 4, core: 2. Of those that a mesh axis runs over, the one named last changes fastest.
Arguments:
- frames: bfloat16 [4, 4096, 1024], P('rec', 'tm'), may hold values from -6 to 6
- lengths: int32 [4], P('rec'), may hold values from 1024 to 4096, as said below
- norm_gain: float32 [1024], replicated, may hold values from 0.1 to 1.9
- memory_gain: float32 [1024], replicated, may hold values from 0.1 to 1.9
- qkv_weight: bfloat16 [3, 1024, 1024], P(None, None, 'tm'), may hold values from -3.75 to 3.75
- out_weight: bfloat16 [1024, 1024], P(None, 'tm'), may hold values from -0.1875 to 0.1875
- segment_ids: int32 [4, 8, 512], P('rec', 'tm'), may hold values from 0 to 127, never falling along the last dimension, each value on 1 to 12 neighbouring positions
- owners: int32 [4, 8, 128, 1], P('rec', 'tm'), may hold values from 0 to 7; in each aligned block of 128 rows (0 to 127, 128 to 255, ..., all dimensions but the last counted through in order) at most 32 rows name the same one
- language_weight: bfloat16 [1024, 2048], P(None, 'rec'), may hold values from -0.1875 to 0.1875
Outputs:
- encoded: bfloat16 [4, 4096, 1024], P('rec', 'tm')
- lm_rows: bfloat16 [4, 8, 256, 2048], P('rec', 'tm')
Inputs may be any that keep to these rules, and one draw needn't show every extreme that they name: `lengths`: one recording has exactly 4096 live frames. `segment_ids`: in each block, token numbers never fall and each of the 128 tokens has 1 to 12 frames, one exactly 12. `owners`: within the 128 tokens of one block no owner is named more than 32 times, a bound that some block reaches.
All inputs are finite; a program needn't handle non-finite values.
Results may differ from a plain program's by a relative error of at most 0.035.
Values may be sent and summed in bfloat16 or wider, within the bound.
No kernel may reach another device: no remote copies, remote signals or barrier semaphores. Data moves between devices by JAX's collectives and lax.ppermute only.
A program may use at most 64 MiB of HBM per device.

v0:
```python
import jax
import jax.numpy as jnp
from jax import lax
from jax.sharding import PartitionSpec as P

H = 16
C = 32
RC = 8
EPS_NORM = 1e-05
EPS_MEMORY = 1e-06
NEG_BIG = -1e30


def shifted(block, axis, distance):
    devices = range(lax.axis_size(axis))
    route = [(i - distance, i) for i in devices if i - distance in devices]
    return lax.ppermute(block, axis, route)


def layer_norm(values_in, gain):
    values_in = values_in.astype(jnp.float32)
    centre = jnp.mean(values_in, axis=-1, keepdims=True)
    centred = values_in - centre
    spread = jnp.mean(centred * centred, axis=-1, keepdims=True)
    return centred * lax.rsqrt(spread + EPS_NORM) * gain


def span_memory(normed, live_mask, gain, span_len):
    model_width = normed.shape[1]
    masked = jnp.where(live_mask[:, None], normed.astype(jnp.float32), jnp.float32(0.0))
    owner_sums = masked.reshape(-1, span_len, model_width).sum(axis=1)
    counts = live_mask.reshape(-1, span_len).astype(jnp.float32).sum(axis=1)
    means = owner_sums / jnp.maximum(counts, 1.0)[:, None]
    power = jnp.mean(means * means, axis=-1, keepdims=True)
    return (means * lax.rsqrt(power + EPS_MEMORY) * gain).astype(jnp.bfloat16)


def block_size():
    return 256


def local_part(query, keys, values, first_frame, length, head_count, span_len, right_len):
    frame_count, model_width = query.shape
    head_size = model_width // head_count
    group_rows = 4 * span_len
    group_count = frame_count // group_rows
    block_rows = block_size()
    query_blocks = query.reshape(group_count, group_rows, head_count, head_size)
    key_blocks = keys[:frame_count].reshape(group_count, group_rows, head_count, head_size)
    value_blocks = values[:frame_count].reshape(group_count, group_rows, head_count, head_size)
    key_tail = keys[frame_count:].reshape(1, right_len, head_count, head_size)
    value_tail = values[frame_count:].reshape(1, right_len, head_count, head_size)
    key_all = jnp.concatenate(
        [key_blocks, jnp.concatenate([key_blocks[1:, :right_len], key_tail], axis=0)], axis=1
    )
    value_all = jnp.concatenate(
        [value_blocks, jnp.concatenate([value_blocks[1:, :right_len], value_tail], axis=0)], axis=1
    )
    start_offsets = jnp.arange(group_count, dtype=jnp.int32)[:, None] * group_rows
    query_pos = first_frame + start_offsets + jnp.arange(group_rows, dtype=jnp.int32)[None, :]
    key_pos = first_frame + jnp.concatenate(
        [
            start_offsets + jnp.arange(group_rows, dtype=jnp.int32)[None, :],
            start_offsets + group_rows + jnp.arange(right_len, dtype=jnp.int32)[None, :],
        ],
        axis=1,
    )
    query_span = query_pos // span_len
    span_end = (query_span + 1) * span_len
    same = (key_pos // span_len)[:, None, :] == query_span[:, :, None]
    ahead = (key_pos[:, None, :] >= span_end[:, :, None]) & (
        key_pos[:, None, :] < span_end[:, :, None] + right_len
    )
    allowed = (same | ahead) & (key_pos < length)[:, None, :]
    scores = jnp.einsum(
        "gqhd,gkhd->ghqk", query_blocks, key_all, preferred_element_type=jnp.float32
    ) * head_size ** (-0.5)
    scores = jnp.where(allowed[:, None], scores, NEG_BIG)
    row_peak = jnp.max(scores, axis=-1)
    weights = jnp.where(allowed[:, None], jnp.exp(scores - row_peak[..., None]), jnp.float32(0.0))
    row_total = jnp.sum(weights, axis=-1)
    accum = jnp.einsum(
        "ghqk,gkhd->ghqd",
        weights.astype(jnp.bfloat16),
        value_all,
        preferred_element_type=jnp.float32,
    )
    block_count = frame_count // block_rows
    row_peak = (
        row_peak.transpose(1, 0, 2).reshape(head_count, block_count, block_rows).transpose(1, 0, 2)
    )
    row_total = (
        row_total.transpose(1, 0, 2).reshape(head_count, block_count, block_rows).transpose(1, 0, 2)
    )
    accum = (
        accum.transpose(1, 0, 2, 3)
        .reshape(head_count, block_count, block_rows, head_size)
        .transpose(1, 0, 2, 3)
    )
    return (row_peak, row_total, accum)


def memory_update(
    carry, memory_keys, memory_values, query, first_frame, length, head_count, span_len
):
    row_peak, row_total, accum = carry
    block_count, _, block_rows = row_peak.shape
    row_count, model_width = memory_keys.shape
    head_size = model_width // head_count
    mem_keys = memory_keys.reshape(row_count, head_count, head_size)
    mem_values = memory_values.reshape(row_count, head_count, head_size)
    mem_index = jnp.arange(row_count, dtype=jnp.int32)
    mem_live = mem_index * span_len < length
    query_blocks = query.reshape(block_count, block_rows, head_count, head_size)
    positions = first_frame + jnp.arange(block_count * block_rows, dtype=jnp.int32).reshape(
        block_count, block_rows
    )

    def one_block(packed):
        query_now, pos_now, peak_now, total_now, accum_now = packed
        scores = jnp.einsum(
            "qhd,khd->hqk", query_now, mem_keys, preferred_element_type=jnp.float32
        ) * head_size ** (-0.5)
        allowed = (mem_index[None, :] < (pos_now // span_len)[:, None]) & mem_live[None, :]
        scores = jnp.where(allowed[None], scores, NEG_BIG)
        new_peak = jnp.maximum(peak_now, jnp.max(scores, axis=-1))
        weights = jnp.where(allowed[None], jnp.exp(scores - new_peak[..., None]), jnp.float32(0.0))
        factor = jnp.exp(peak_now - new_peak)
        total_next = total_now * factor + jnp.sum(weights, axis=-1)
        accum_next = accum_now * factor[..., None] + jnp.einsum(
            "hqk,khd->hqd",
            weights.astype(jnp.bfloat16),
            mem_values,
            preferred_element_type=jnp.float32,
        )
        return (new_peak, total_next, accum_next)

    return lax.map(one_block, (query_blocks, positions, row_peak, row_total, accum))


def finish(carry, frame_count, model_width):
    row_peak, row_total, accum = carry
    result = accum / row_total[..., None]
    return result.transpose(0, 2, 1, 3).reshape(frame_count, model_width).astype(jnp.bfloat16)


def dispatch_matrix(owner_ids, owner_count, capacity):
    choose = (owner_ids[:, None] == jnp.arange(owner_count, dtype=jnp.int32)[None, :]).astype(
        jnp.int32
    )
    before = jnp.cumsum(choose, axis=0) - choose
    slot_index = jnp.sum(before * choose, axis=1)
    target = owner_ids * capacity + slot_index
    slot_rows = jnp.arange(owner_count * capacity, dtype=jnp.int32)
    return (slot_rows[:, None] == target[None, :]).astype(jnp.bfloat16)


def per_device(
    frames,
    lengths,
    norm_gain,
    memory_gain,
    qkv_weight,
    out_weight,
    segment_ids,
    owners,
    language_weight,
):
    local_frames = frames[0]
    frame_count, model_width = local_frames.shape
    head_count = H
    time_count = lax.axis_size("tm")
    first_frame = lax.axis_index("tm") * frame_count
    length = lengths[0]
    live_mask = first_frame + jnp.arange(frame_count, dtype=jnp.int32) < length
    right_frames = shifted(local_frames[:RC], "tm", -1)
    normed = layer_norm(local_frames, norm_gain).astype(jnp.bfloat16)
    normed_right = layer_norm(right_frames, norm_gain).astype(jnp.bfloat16)
    memory = span_memory(normed, live_mask, memory_gain, C)
    stacked_rows = jnp.concatenate([normed, normed_right, memory], axis=0)
    projected = jnp.einsum(
        "fd,kdw->kfw",
        stacked_rows,
        lax.all_gather(qkv_weight, "tm", axis=2, tiled=True),
        preferred_element_type=jnp.float32,
    ).astype(jnp.bfloat16)
    split_at = frame_count + RC
    query = projected[0, :frame_count]
    keys = projected[1, :split_at]
    values = projected[2, :split_at]
    memory_keys = projected[1, split_at:]
    memory_values = projected[2, split_at:]
    carry = local_part(query, keys, values, first_frame, length, head_count, C, RC)
    carry = memory_update(
        carry,
        lax.all_gather(memory_keys, "tm", axis=0, tiled=True),
        lax.all_gather(memory_values, "tm", axis=0, tiled=True),
        query,
        first_frame,
        length,
        head_count,
        C,
    )
    attended = finish(carry, frame_count, model_width)
    output_proj = jnp.dot(
        attended,
        lax.all_gather(out_weight, "tm", axis=1, tiled=True),
        preferred_element_type=jnp.float32,
    )
    encoded = jnp.where(
        live_mask[:, None], local_frames.astype(jnp.float32) + output_proj, jnp.float32(0.0)
    ).astype(jnp.bfloat16)
    token_count = owners.shape[2]
    segments = segment_ids[0, 0]
    owner_indicator = (
        segments[None, :] == jnp.arange(token_count, dtype=jnp.int32)[:, None]
    ).astype(jnp.bfloat16)
    owner_sums = jnp.dot(owner_indicator, encoded, preferred_element_type=jnp.float32)
    counts = jnp.sum(owner_indicator.astype(jnp.float32), axis=1)
    pooled_rows = (owner_sums / counts[:, None]).astype(jnp.bfloat16)
    slot_count = 2 * token_count
    capacity = slot_count // time_count
    route_matrix = dispatch_matrix(owners[0, 0, :, 0], time_count, capacity)
    sent_rows = jnp.dot(route_matrix, pooled_rows, preferred_element_type=jnp.float32).astype(
        jnp.bfloat16
    )
    received = lax.all_to_all(
        sent_rows.reshape(time_count, capacity, model_width),
        "tm",
        split_axis=0,
        concat_axis=0,
        tiled=True,
    )
    received = received.reshape(slot_count, model_width)
    lm_out = jnp.dot(
        received,
        lax.all_gather(language_weight, "rec", axis=1, tiled=True),
        preferred_element_type=jnp.float32,
    ).astype(jnp.bfloat16)
    return (encoded[None], lm_out[None, None])


def solution(mesh):
    in_specs = (
        P("rec", "tm", None),
        P("rec"),
        P(),
        P(),
        P(None, None, "tm"),
        P(None, "tm"),
        P("rec", "tm", None),
        P("rec", "tm", None, None),
        P(None, "rec"),
    )
    out_specs = (P("rec", "tm", None), P("rec", "tm", None, None))
    return jax.shard_map(
        per_device, mesh=mesh, in_specs=in_specs, out_specs=out_specs, check_vma=False
    )
```

profile of v0, /device:TPU:0, one launch (start us, length us, event | category | flops | bytes accessed | tf_op | source)
XLA Modules:
  0.0 270.1 jit_solution(14263593374666861622)
XLA Ops:
  9.4 1.3 collective-permute-start
  16.4 95.8 %all-gather.6.cloned.1.call-done = bf16[3,1024,1024]{2,1,0:T(8,128)(2,1)} async-done(((bf16[3,1024,128]{2,1,0:T(8,128)(2,1)}), bf16[3,1024,1024]{2,1,0:T(8,128)(2,1)}) %all-gather.6.cloned.1.call-update) | async-done | bytes 6291472 | tf_op jit(solution)/shard_map/all_gather | solution.py:184
  112.3 6.8 %convert_bitcast_fusion = bf16[3,536,1024]{2,1,0:T(8,128)(2,1)S(1)} fusion(bf16[3,1024,1024]{2,1,0:T(8,128)(2,1)} %all-gather.6.cloned.1.call-done, bf16[16,1024]{1,0:T(8,128)(2,1)S(1)} %multiply_convert_fusion.2, bf16[8,1024]{1,0:T(8,128)(2,1)S(1)} %fusion.75, bf16[512,1024]{1,0:T(8,128)(2,1)S(1)} %multiply_convert_fusion.1), kind=kOutput, calls=%fused_computation.46 | convolution fusion | flops 3377160192 | bytes 10682368 | tf_op jit(solution)/shard_map/fd,kdw->kfw/dot_general | solution.py:181
  119.1 1.9 fusion.88
  121.5 2.3 reshape.439
  123.8 2.3 reshape.440
  126.1 1.4 fusion.87
  127.5 3.0 %reshape.441 = bf16[4,128,16,64]{3,2,1,0:T(8,128)(2,1)S(1)} reshape(bf16[1,512,1024]{2,1,0:T(8,128)(2,1)} %get-tuple-element.258) | data formatting | bytes 2097152 | tf_op jit(solution)/shard_map/reshape | solution.py:49
  130.5 2.5 copy.70
  132.9 2.1 slice.56
  135.3 3.0 %reshape.442 = bf16[4,128,16,64]{3,2,1,0:T(8,128)(2,1)S(1)} reshape(bf16[1,512,1024]{2,1,0:T(8,128)(2,1)} %get-tuple-element.257) | data formatting | bytes 2097152 | tf_op jit(solution)/shard_map/reshape | solution.py:50
  138.2 2.5 copy.79
  140.7 1.2 slice.60
  142.1 3.6 %fusion.29 = (f32[4,16,128]{2,1,0:T(8,128)S(1)}, f32[4,16,128,136]{2,3,1,0:T(8,128)S(1)}) fusion(pred[4,128,136]{1,2,0:T(8,128)(4,1)S(1)} %or_and_fusion, bf16[1,8,16,64]{1,3,2,0:T(8,128)(2,1)S(1)} %bitcast.115, bf16[3,8,16,64]{1,3,2,0:T(8,128)(2,1)} %slice.56, bf16[4,128,16,64]{1,3,2,0:T(8,128)(2,1)} %copy.70, bf16[4,128,16,64]{3,2,1,0:T(8,128)(2,1)} %reshape.439), kind=kOutput, calls=%fused_computation.45 | convolution fusion | flops 149282816 | bytes 6721536 | tf_op jit(solution)/shard_map/gqhd,gkhd->ghqk/dot_general | solution.py:75
  145.7 1.3 fusion.31
  147.0 1.4 fusion.54
  148.4 2.7 %copy.80 = f32[16,4,128,64]{2,1,3,0:T(4,128)} copy(f32[16,4,128,64]{2,3,0,1:T(8,128)S(1)} %fusion.54) | data formatting | bytes 4194304 | tf_op jit(solution)/shard_map/transpose | solution.py:96
  151.2 3.1 %reshape.429 = f32[16,2,256,64]{2,1,3,0:T(2,128)S(1)} reshape(f32[16,4,128,64]{2,1,3,0:T(4,128)} %copy.80) | data formatting | bytes 4194304 | tf_op jit(solution)/shard_map/reshape | solution.py:97
  154.4 3.6 %copy.84 = bf16[2,256,16,64]{1,3,2,0:T(8,128)(2,1)} copy(bf16[2,256,16,64]{3,2,1,0:T(8,128)(2,1)} %reshape.440) | data formatting | bytes 2097152
  158.0 32.7 %all-gather = bf16[1,128,1024]{2,1,0:T(8,128)(2,1)} all-gather(bf16[1,16,1024]{2,1,0:T(8,128)(2,1)S(1)} %copy-done.6), channel_id=2, replica_groups=mesh['rec'=4,'tm'=8] {'tm'}, dimensions={1}, use_global_device_ids=true | all-gather | bytes 294912 | tf_op jit(solution)/shard_map/all_gather | solution.py:196
  190.8 1.1 copy.75
  191.9 32.8 %all-gather.1 = bf16[1,128,1024]{2,1,0:T(8,128)(2,1)} all-gather(bf16[1,16,1024]{2,1,0:T(8,128)(2,1)S(1)} %get-tuple-element.255), channel_id=3, replica_groups=mesh['rec'=4,'tm'=8] {'tm'}, dimensions={1}, use_global_device_ids=true | all-gather | bytes 294912 | tf_op jit(solution)/shard_map/all_gather | solution.py:197
  224.6 1.8 copy.81
  226.4 11.6 %while.15 = (s32[]{:T(128)}, f32[2,16,256]{2,1,0:T(8,128)S(1)}, f32[2,16,256,64]{2,3,1,0:T(8,128)}, f32[2,16,256]{2,0,1:T(2,128)S(1)}, f32[2,16,256]{2,0,1:T(2,1...) while((s32[]{:T(128)}, f32[2,16,256]{2,1,0:T(8,128)S(1)}, ...), condition=%wide.region_12.13_spmd.clone, body=%wide.region_9.12_spmd.clone.sunk | while | flops 141643776 | bytes 29792224 | solution.py:138
  227.2 1.7 fusion.111
  233.0 1.7 fusion.111
  238.0 1.8 fusion.64
  241.3 2.9 %fusion.53 = bf16[512,1024]{1,0:T(8,128)(2,1)S(1)} fusion(bf16[1,512,1024]{2,1,0:T(8,128)(2,1)S(1)} %copy-done, bf16[512,1024]{0,1:T(8,128)(2,1)S(1)} %bitcast.110, bf16[1024,1024]{1,0:T(8,128)(2,1)} %all-gather.8.cloned.1.call-done, pred[512]{0:T(512)(128)(4,1)S(1)} %copy-done.14), kind=kOutput, calls=%fused_computation.72 | convolution fusion | flops 1075838976 | bytes 5243392 | tf_op jit(solution)/shard_map/dot_general | solution.py:205
  244.1 1.3 convolution_convert_fusion.1
  245.5 3.5 %all-to-all-start = ((bf16[8,32,1024]{2,1,0:T(8,128)(2,1)}), bf16[8,32,1024]{2,1,0:T(8,128)(2,1)S(1)}, u32[]{:S(2)}, u32[]{:S(2)}) async-start(bf16[8,32,1024]{2,1,0:T(8,128)(2,1)} %bitcast.20), calls=%async_computation | async-start | bytes 1048576 | tf_op jit(solution)/shard_map/all_to_all | solution.py:227
  249.0 10.2 %all-to-all-done = bf16[8,32,1024]{2,1,0:T(8,128)(2,1)S(1)} async-done(((bf16[8,32,1024]{2,1,0:T(8,128)(2,1)}), bf16[8,32,1024]{2,1,0:T(8,128)(2,1)S(1)}, u32[]{:S(2)}, u32[]{:S(2)}) %all-to-all-start) | async-done | bytes 524320 | tf_op jit(solution)/shard_map/all_to_all | solution.py:227
  259.2 4.4 %fusion.32 = bf16[1,1,256,2048]{3,2,1,0:T(8,128)(2,1)} fusion(bf16[256,1024]{1,0:T(8,128)(2,1)S(1)} %bitcast.111, bf16[1024,2048]{1,0:T(8,128)(2,1)} %all-gather.10.cloned.1.call-done), kind=kOutput, calls=%fused_computation.50 | convolution fusion | flops 1074266112 | bytes 5767168 | tf_op jit(solution)/shard_map/dot_general | solution.py:235
  (112 shorter events, 17.4 us)
Async XLA Ops:
  7.2 3.6 %copy-start = (bf16[1,512,1024]{2,1,0:T(8,128)(2,1)S(1)}, bf16[1,512,1024]{2,1,0:T(8,128)(2,1)}, u32[]{:S(2)}) copy-start(bf16[1,512,1024]{2,1,0:T(8,128)(2,1)} %param.11) | copy-start | bytes 3145732
  7.2 5.2 %copy-start.7 = (f32[1024]{0:T(1024)S(1)}, f32[1024]{0:T(1024)}, u32[]{:S(2)}) copy-start(f32[1024]{0:T(1024)} %param.13) | copy-start | bytes 12292
  7.2 105.1 %all-gather.6.cloned.1.call-start = ((), (), s32[]{:S(2)}) async-start(), calls=%async_computation.1 | async-start | bytes 7077888 | tf_op jit(solution)/shard_map/all_gather | solution.py:184
  7.9 233.3 %all-gather.8.cloned.1.call-start = ((), (), s32[]{:S(2)}) async-start(), calls=%async_computation.2 | async-start | bytes 2359296 | tf_op jit(solution)/shard_map/all_gather | solution.py:207
  8.7 240.3 %all-gather.10.cloned.1.call-start = ((), (), s32[]{:S(2)}) async-start(), calls=%async_computation.3 | async-start | bytes 5242880 | tf_op jit(solution)/shard_map/all_gather | solution.py:237
  9.4 6.6 %collective-permute-start = (bf16[8,1024]{1,0:T(8,128)(2,1)S(1)}, bf16[8,1024]{1,0:T(8,128)(2,1)S(1)}, u32[]{:S(2)}, u32[]{:S(2)}) collective-permute-start(bf16[8,1024]{1,0:T(8,128)(2,1)S(1)} %slice_bitcast_fusion), channel_id=1, source_target_pairs={{1,0},{2,1},{3,2},{4,3},{5,4},{6,5},{7,6},{9,8},{10,9},{11,10},{12... | collective-permute-start | bytes 49160 | tf_op jit(solution)/shard_map/ppermute | solution.py:17
  11.0 3.0 %copy-start.10 = (s32[1,1,128,1]{2,3,1,0:T(1,128)S(1)}, s32[1,1,128,1]{2,3,1,0:T(1,128)}, u32[]{:S(2)}) copy-start(s32[1,1,128,1]{2,3,1,0:T(1,128)} %param.18) | copy-start | bytes 1540
  11.4 3.5 %copy-start.11 = (s32[1,1,512]{2,1,0:T(1,128)S(1)}, s32[1,1,512]{2,1,0:T(1,128)}, u32[]{:S(2)}) copy-start(s32[1,1,512]{2,1,0:T(1,128)} %param.17) | copy-start | bytes 6148
  11.4 3.6 %copy-start.9 = (f32[1024]{0:T(1024)S(1)}, f32[1024]{0:T(1024)}, u32[]{:S(2)}) copy-start(f32[1024]{0:T(1024)} %param.14) | copy-start | bytes 12292
  119.1 2.4 copy-start.2
  145.7 1.3 copy-start.1
  154.3 3.7 %copy-start.6 = (bf16[1,16,1024]{2,1,0:T(8,128)(2,1)S(1)}, bf16[1,16,1024]{2,1,0:T(8,128)(2,1)}, u32[]{:S(2)}) copy-start(bf16[1,16,1024]{2,1,0:T(8,128)(2,1)} %get-tuple-element.256) | copy-start | bytes 98308
  154.4 72.0 %copy-start.8 = (f32[2,16,256]{2,1,0:T(8,128)S(1)}, f32[2,16,256]{2,1,0:T(8,128)}, u32[]{:S(2)}) copy-start(f32[2,16,256]{2,1,0:T(8,128)} %custom-call) | copy-start | bytes 98308
  227.2 2.9 %copy-start.3 = (f32[2,16,256,64]{2,3,1,0:T(8,128)S(1)}, f32[2,16,256,64]{2,3,1,0:T(8,128)}, u32[]{:S(2)}) copy-start(f32[2,16,256,64]{2,3,1,0:T(8,128)} %get-tuple-element.360) | copy-start | bytes 6291460 | tf_op jit(solution)/shard_map/while
  227.2 2.9 %copy-start.5 = (bf16[128,16,64]{0,2,1:T(8,128)(2,1)S(1)}, bf16[128,16,64]{0,2,1:T(8,128)(2,1)}, u32[]{:S(2)}) copy-start(bf16[128,16,64]{0,2,1:T(8,128)(2,1)} %get-tuple-element.379) | copy-start | bytes 786436 | tf_op jit(solution)/shard_map/while
  230.8 1.4 copy-start.4
  233.0 2.9 %copy-start.3 = (f32[2,16,256,64]{2,3,1,0:T(8,128)S(1)}, f32[2,16,256,64]{2,3,1,0:T(8,128)}, u32[]{:S(2)}) copy-start(f32[2,16,256,64]{2,3,1,0:T(8,128)} %get-tuple-element.360) | copy-start | bytes 6291460 | tf_op jit(solution)/shard_map/while
  233.0 2.9 %copy-start.5 = (bf16[128,16,64]{0,2,1:T(8,128)(2,1)S(1)}, bf16[128,16,64]{0,2,1:T(8,128)(2,1)}, u32[]{:S(2)}) copy-start(bf16[128,16,64]{0,2,1:T(8,128)(2,1)} %get-tuple-element.379) | copy-start | bytes 786436 | tf_op jit(solution)/shard_map/while
  236.6 1.4 copy-start.4
  239.9 1.4 copy-start.14
  241.2 2.9 %copy-start.13 = (s32[128]{0:T(128)S(1)}, s32[128]{0:T(128)}, u32[]{:S(2)}) copy-start(s32[128]{0:T(128)} %multiply_add_fusion) | copy-start | bytes 1540
  244.1 19.5 %copy-start.12 = (bf16[512,1024]{1,0:T(8,128)(2,1)}, bf16[512,1024]{1,0:T(8,128)(2,1)S(1)}, u32[]{:S(2)}) copy-start(bf16[512,1024]{1,0:T(8,128)(2,1)S(1)} %fusion.53) | copy-start | bytes 3145732
  245.5 13.7 %all-to-all-start = ((bf16[8,32,1024]{2,1,0:T(8,128)(2,1)}), bf16[8,32,1024]{2,1,0:T(8,128)(2,1)S(1)}, u32[]{:S(2)}, u32[]{:S(2)}) async-start(bf16[8,32,1024]{2,1,0:T(8,128)(2,1)} %bitcast.20), calls=%async_computation | async-start | bytes 1048576 | tf_op jit(solution)/shard_map/all_to_all | solution.py:227
Sparse Core Ops, SparseCore 0:
  10.0 102.1 all-gather.5
  114.3 48.8 all-gather.7
  164.8 32.6 all-gather.9
where the time goes:
time: 271 us; the launch traced here: 270 us
  waiting for transfers between devices  107 us (39%)
  blocking collectives  65.5 us (24%)
  local copies, waits for them, and re-layouts  41.5 us (15%)
  matrix products  25.3 us (9%)
  between operations  14.8 us (5%)
  other arithmetic  10.5 us (4%)
  starting transfers between devices  4.89 us (2%)
    all_gather x1, waiting for transfers between devices, per_device(): lax.all_gather(qkv_weight, 'tm', axis=2, tiled=True)  95.8 us
    all_gather x1, blocking collectives, per_device(): lax.all_gather(memory_values, 'tm', axis=0, tiled=True)  32.8 us
    all_gather x1, blocking collectives, per_device(): lax.all_gather(memory_keys, 'tm', axis=0, tiled=True)  32.7 us
    all_to_all x1, waiting for transfers between devices, per_device(): lax.all_to_all(sent_rows.reshape(time_count, capacity, model_width), 'tm'...  10.2 us
    dot_general x1, matrix products, per_device(): jnp.einsum('fd,kdw->kfw', stacked_rows, lax.all_gather(qkv_weight, 'tm',...  6.85 us
    reshape x2, local copies, waits for them, and re-layouts, local_part(): values[:frame_count].reshape(group_count, group_rows, head_count, head_size)  5.43 us
    reshape x2, local copies, waits for them, and re-layouts, local_part(): keys[:frame_count].reshape(group_count, group_rows, head_count, head_size)  5.42 us
  transfers between devices with their start and end apart: 5, of which 2 were waited for; matrix products, arithmetic and copies ran while one was open for 26% of the time, Pallas kernels for 0%

commit v1 on v0

--- a/solution.py
+++ b/solution.py
@@ -9,6 +9,23 @@
 EPS_NORM = 1e-05
 EPS_MEMORY = 1e-06
 NEG_BIG = -1e30
+
+
+def in_order(parts, dim):
+    dims = list(parts.shape[1:])
+    dims[dim] *= parts.shape[0]
+    return jnp.moveaxis(parts, 0, dim).reshape(dims)
+
+
+def collect(shard, axis, dim):
+    devices = lax.axis_size(axis)
+    ahead = [(i, (i + 1) % devices) for i in range(devices)]
+    parts = [shard]
+    while len(parts) < devices:
+        parts.append(lax.ppermute(parts[-1], axis, ahead))
+    index = lax.axis_index(axis)
+    parts = jnp.stack(parts)[(index - jnp.arange(devices)) % devices]
+    return in_order(parts, dim)
 
 
 def shifted(block, axis, distance):
@@ -194,7 +211,7 @@
     carry = memory_update(
         carry,
         lax.all_gather(memory_keys, "tm", axis=0, tiled=True),
-        lax.all_gather(memory_values, "tm", axis=0, tiled=True),
+        collect(memory_values, "tm", 0),
         query,
         first_frame,
         length,

time: 271 us -> 291 us (1.074)
  waiting for transfers between devices: 107 us -> 142 us
  blocking collectives: 65.5 us -> 33.3 us
  local copies, waits for them, and re-layouts: 41.5 us -> 55.4 us
    ppermute x0 -> x7, waiting for transfers between devices: none -> 34.8 us  [collect(): parts.append(lax.ppermute(parts[-1], axis, ahead))]
    all_gather x1 -> x0, blocking collectives: 32.8 us -> none  [per_device(): lax.all_gather(memory_values, 'tm', axis=0, tiled=True)]
    unnamed x26 -> x37, local copies, waits for them, and re-layouts: 4.34 us -> 10.6 us
  transfers between devices with their start and end apart: 5 -> 12, of which waited for: 2 -> 8; matrix products, arithmetic and copies ran while one was open for 26% -> 30% of each run, Pallas kernels for 0% -> 0%
where the time goes in v1:
time: 291 us; the launch traced here: 290 us
  waiting for transfers between devices  142 us (49%)
  local copies, waits for them, and re-layouts  55.4 us (19%)
  blocking collectives  33.3 us (11%)
  matrix products  26.3 us (9%)
  between operations  14.8 us (5%)
  other arithmetic  11.1 us (4%)
  starting transfers between devices  7.19 us (2%)
    all_gather x1, waiting for transfers between devices, per_device(): lax.all_gather(qkv_weight, 'tm', axis=2, tiled=True)  95.6 us
    ppermute x7, waiting for transfers between devices, collect(): parts.append(lax.ppermute(parts[-1], axis, ahead))  34.8 us
    all_gather x1, blocking collectives, per_device(): lax.all_gather(memory_keys, 'tm', axis=0, tiled=True)  33.3 us
    unnamed x37, local copies, waits for them, and re-layouts  10.6 us
    all_to_all x1, waiting for transfers between devices, per_device(): lax.all_to_all(sent_rows.reshape(time_count, capacity, model_width), 'tm'...  10.2 us
    reshape x2, local copies, waits for them, and re-layouts, local_part(): keys[:frame_count].reshape(group_count, group_rows, head_count, head_size)  7.53 us
    dot_general x1, matrix products, per_device(): jnp.einsum('fd,kdw->kfw', stacked_rows, lax.all_gather(qkv_weight, 'tm',...  6.88 us
    reshape x2, local copies, waits for them, and re-layouts, local_part(): values[:frame_count].reshape(group_count, group_rows, head_count, head_size)  5.94 us
  transfers between devices with their start and end apart: 12, of which 8 were waited for; matrix products, arithmetic and copies ran while one was open for 30% of the time, Pallas kernels for 0%

profile of v1, /device:TPU:0, one launch (start us, length us, event | category | flops | bytes accessed | tf_op | source)
XLA Modules:
  0.0 290.3 jit_solution(3535735185126601836)
XLA Ops:
  17.1 95.6 %all-gather.5.cloned.1.call-done = bf16[3,1024,1024]{2,1,0:T(8,128)(2,1)} async-done(((bf16[3,1024,128]{2,1,0:T(8,128)(2,1)}), bf16[3,1024,1024]{2,1,0:T(8,128)(2,1)}) %all-gather.5.cloned.1.call-update) | async-done | bytes 6291472 | tf_op jit(solution)/shard_map/all_gather | solution.py:201
  112.6 6.9 %convert_bitcast_fusion = bf16[3,536,1024]{2,1,0:T(8,128)(2,1)S(1)} fusion(bf16[3,1024,1024]{2,1,0:T(8,128)(2,1)} %all-gather.5.cloned.1.call-done, bf16[16,1024]{1,0:T(8,128)(2,1)S(1)} %multiply_convert_fusion.2, bf16[8,1024]{1,0:T(8,128)(2,1)S(1)} %fusion.75, bf16[512,1024]{1,0:T(8,128)(2,1)S(1)} %multiply_convert_fusion.1), kind=kOutput, calls=%fused_computation.47 | convolution fusion | flops 3377160192 | bytes 10682368 | tf_op jit(solution)/shard_map/fd,kdw->kfw/dot_general | solution.py:198
  122.9 4.0 %reshape.492 = bf16[4,128,16,64]{3,2,1,0:T(8,128)(2,1)} reshape(bf16[1,512,1024]{2,1,0:T(8,128)(2,1)} %get-tuple-element.259) | data formatting | bytes 2097152 | tf_op jit(solution)/shard_map/reshape | solution.py:66
  126.9 3.5 %copy.70 = bf16[4,128,16,64]{1,3,2,0:T(8,128)(2,1)} copy(bf16[4,128,16,64]{3,2,1,0:T(8,128)(2,1)} %reshape.492) | data formatting | bytes 2097152 | tf_op jit(solution)/shard_map/reshape | solution.py:66
  130.4 2.1 slice.58
  132.5 2.3 reshape.490
  135.0 2.3 reshape.493
  137.3 3.6 %copy.79 = bf16[4,128,16,64]{1,3,2,0:T(8,128)(2,1)} copy(bf16[4,128,16,64]{3,2,1,0:T(8,128)(2,1)} %reshape.493) | data formatting | bytes 2097152 | tf_op jit(solution)/shard_map/reshape | solution.py:67
  141.0 2.1 slice.62
  143.9 3.3 %fusion.29 = (f32[4,16,128]{2,1,0:T(8,128)S(1)}, f32[4,16,128,136]{2,3,1,0:T(8,128)S(1)}) fusion(pred[4,128,136]{1,2,0:T(8,128)(4,1)S(1)} %or_and_fusion, bf16[1,8,16,64]{1,3,2,0:T(8,128)(2,1)S(1)} %bitcast.131, bf16[3,8,16,64]{1,3,2,0:T(8,128)(2,1)} %slice.58, bf16[4,128,16,64]{1,3,2,0:T(8,128)(2,1)S(1)} %copy-done.1, bf16[4,128,16,64]{3,2,1,0:T(8,128)(2,1)} %reshape.490), kind=kOutput, calls=%fused_computation.46 | convolution fusion | flops 149282816 | bytes 6721536 | tf_op jit(solution)/shard_map/gqhd,gkhd->ghqk/dot_general | solution.py:92
  148.7 2.7 fusion.54
  151.4 33.3 %all-gather = bf16[1,128,1024]{2,1,0:T(8,128)(2,1)} all-gather(bf16[1,16,1024]{2,1,0:T(8,128)(2,1)S(1)} %get-tuple-element.257), channel_id=2, replica_groups=mesh['rec'=4,'tm'=8] {'tm'}, dimensions={1}, use_global_device_ids=true | all-gather | bytes 294912 | tf_op jit(solution)/shard_map/all_gather | solution.py:213
  184.7 2.3 reshape.491
  187.0 4.4 %copy.80 = f32[16,4,128,64]{2,1,3,0:T(4,128)} copy(f32[16,4,128,64]{2,3,0,1:T(8,128)} %fusion.54) | data formatting | bytes 4194304 | tf_op jit(solution)/shard_map/transpose | solution.py:113
  191.4 3.1 %reshape.475 = f32[16,2,256,64]{2,1,3,0:T(2,128)S(1)} reshape(f32[16,4,128,64]{2,1,3,0:T(4,128)} %copy.80) | data formatting | bytes 4194304 | tf_op jit(solution)/shard_map/reshape | solution.py:114
  194.7 3.6 %copy.83 = bf16[2,256,16,64]{1,3,2,0:T(8,128)(2,1)} copy(bf16[2,256,16,64]{3,2,1,0:T(8,128)(2,1)} %reshape.491) | data formatting | bytes 2097152
  201.6 4.6 %collective-permute-done.2 = bf16[16,1024]{1,0:T(8,128)(2,1)S(1)} collective-permute-done((bf16[16,1024]{1,0:T(8,128)(2,1)}, bf16[16,1024]{1,0:T(8,128)(2,1)S(1)}, u32[]{:S(2)}, u32[]{:S(2)}) %collective-permute-start.2) | collective-permute-done | bytes 32800 | tf_op jit(solution)/shard_map/ppermute | solution.py:25
  206.9 6.0 %collective-permute-done.3 = bf16[16,1024]{1,0:T(8,128)(2,1)S(1)} collective-permute-done((bf16[16,1024]{1,0:T(8,128)(2,1)S(1)}, bf16[16,1024]{1,0:T(8,128)(2,1)S(1)}, u32[]{:S(2)}, u32[]{:S(2)}) %collective-permute-start.3) | collective-permute-done | bytes 32800 | tf_op jit(solution)/shard_map/ppermute | solution.py:25
  213.5 6.0 %collective-permute-done.4 = bf16[16,1024]{1,0:T(8,128)(2,1)S(1)} collective-permute-done((bf16[16,1024]{1,0:T(8,128)(2,1)S(1)}, bf16[16,1024]{1,0:T(8,128)(2,1)S(1)}, u32[]{:S(2)}, u32[]{:S(2)}) %collective-permute-start.4) | collective-permute-done | bytes 32800 | tf_op jit(solution)/shard_map/ppermute | solution.py:25
  220.1 6.2 %collective-permute-done.5 = bf16[16,1024]{1,0:T(8,128)(2,1)S(1)} collective-permute-done((bf16[16,1024]{1,0:T(8,128)(2,1)S(1)}, bf16[16,1024]{1,0:T(8,128)(2,1)S(1)}, u32[]{:S(2)}, u32[]{:S(2)}) %collective-permute-start.5) | collective-permute-done | bytes 32800 | tf_op jit(solution)/shard_map/ppermute | solution.py:25
  227.0 6.0 %collective-permute-done.6 = bf16[16,1024]{1,0:T(8,128)(2,1)S(1)} collective-permute-done((bf16[16,1024]{1,0:T(8,128)(2,1)S(1)}, bf16[16,1024]{1,0:T(8,128)(2,1)S(1)}, u32[]{:S(2)}, u32[]{:S(2)}) %collective-permute-start.6) | collective-permute-done | bytes 32800 | tf_op jit(solution)/shard_map/ppermute | solution.py:25
  233.6 6.0 %collective-permute-done.7 = bf16[16,1024]{1,0:T(8,128)(2,1)S(1)} collective-permute-done((bf16[16,1024]{1,0:T(8,128)(2,1)S(1)}, bf16[16,1024]{1,0:T(8,128)(2,1)S(1)}, u32[]{:S(2)}, u32[]{:S(2)}) %collective-permute-start.7) | collective-permute-done | bytes 32800 | tf_op jit(solution)/shard_map/ppermute | solution.py:25
  240.2 2.2 gather_fusion
  242.4 2.1 reshape_reshape.3
  244.5 2.1 copy.85
  246.6 11.6 %while.15 = (s32[]{:T(128)}, f32[2,16,256]{2,1,0:T(8,128)S(1)}, f32[2,16,256,64]{2,3,1,0:T(8,128)}, f32[2,16,256]{2,0,1:T(2,128)S(1)}, f32[2,16,256]{2,0,1:T(2,1...) while((s32[]{:T(128)}, f32[2,16,256]{2,1,0:T(8,128)S(1)}, ...), condition=%wide.region_12.13_spmd.clone, body=%wide.region_9.12_spmd.clone.sunk | while | flops 141643776 | bytes 29792224 | solution.py:155
  247.4 1.7 fusion.112
  258.2 1.8 fusion.64
  261.4 2.9 fusion.53
  265.6 3.5 %all-to-all-start = ((bf16[8,32,1024]{2,1,0:T(8,128)(2,1)}), bf16[8,32,1024]{2,1,0:T(8,128)(2,1)S(1)}, u32[]{:S(2)}, u32[]{:S(2)}) async-start(bf16[8,32,1024]{2,1,0:T(8,128)(2,1)} %bitcast.28), calls=%async_computation | async-start | bytes 1048576 | tf_op jit(solution)/shard_map/all_to_all | solution.py:244
  269.2 10.2 %all-to-all-done = bf16[8,32,1024]{2,1,0:T(8,128)(2,1)S(1)} async-done(((bf16[8,32,1024]{2,1,0:T(8,128)(2,1)}), bf16[8,32,1024]{2,1,0:T(8,128)(2,1)S(1)}, u32[]{:S(2)}, u32[]{:S(2)}) %all-to-all-start) | async-done | bytes 524320 | tf_op jit(solution)/shard_map/all_to_all | solution.py:244
  279.3 4.4 %fusion.32 = bf16[1,1,256,2048]{3,2,1,0:T(8,128)(2,1)} fusion(bf16[256,1024]{1,0:T(8,128)(2,1)S(1)} %bitcast.128, bf16[1024,2048]{1,0:T(8,128)(2,1)} %all-gather.9.cloned.1.call-done), kind=kOutput, calls=%fused_computation.51 | convolution fusion | flops 1074266112 | bytes 5767168 | tf_op jit(solution)/shard_map/dot_general | solution.py:252
  (140 shorter events, 34.4 us)
Async XLA Ops:
  7.2 3.6 %copy-start = (bf16[1,512,1024]{2,1,0:T(8,128)(2,1)S(1)}, bf16[1,512,1024]{2,1,0:T(8,128)(2,1)}, u32[]{:S(2)}) copy-start(bf16[1,512,1024]{2,1,0:T(8,128)(2,1)} %param.11) | copy-start | bytes 3145732
  7.2 5.3 %copy-start.8 = (f32[1024]{0:T(1024)S(1)}, f32[1024]{0:T(1024)}, u32[]{:S(2)}) copy-start(f32[1024]{0:T(1024)} %param.13) | copy-start | bytes 12292
  7.2 105.5 %all-gather.5.cloned.1.call-start = ((), (), s32[]{:S(2)}) async-start(), calls=%async_computation.1 | async-start | bytes 7077888 | tf_op jit(solution)/shard_map/all_gather | solution.py:201
  7.9 253.5 %all-gather.7.cloned.1.call-start = ((), (), s32[]{:S(2)}) async-start(), calls=%async_computation.2 | async-start | bytes 2359296 | tf_op jit(solution)/shard_map/all_gather | solution.py:224
  8.7 260.5 %all-gather.9.cloned.1.call-start = ((), (), s32[]{:S(2)}) async-start(), calls=%async_computation.3 | async-start | bytes 5242880 | tf_op jit(solution)/shard_map/all_gather | solution.py:254
  9.4 7.2 %collective-permute-start = (bf16[8,1024]{1,0:T(8,128)(2,1)S(1)}, bf16[8,1024]{1,0:T(8,128)(2,1)S(1)}, u32[]{:S(2)}, u32[]{:S(2)}) collective-permute-start(bf16[8,1024]{1,0:T(8,128)(2,1)S(1)} %slice_bitcast_fusion.1), channel_id=1, source_target_pairs={{1,0},{2,1},{3,2},{4,3},{5,4},{6,5},{7,6},{9,8},{10,9},{11,10},{12... | collective-permute-start | bytes 49160 | tf_op jit(solution)/shard_map/ppermute | solution.py:34
  11.0 3.0 %copy-start.11 = (s32[1,1,128,1]{2,3,1,0:T(1,128)S(1)}, s32[1,1,128,1]{2,3,1,0:T(1,128)}, u32[]{:S(2)}) copy-start(s32[1,1,128,1]{2,3,1,0:T(1,128)} %param.18) | copy-start | bytes 1540
  11.4 3.6 %copy-start.12 = (s32[1,1,512]{2,1,0:T(1,128)S(1)}, s32[1,1,512]{2,1,0:T(1,128)}, u32[]{:S(2)}) copy-start(s32[1,1,512]{2,1,0:T(1,128)} %param.17) | copy-start | bytes 6148
  11.4 4.3 %copy-start.10 = (f32[1024]{0:T(1024)S(1)}, f32[1024]{0:T(1024)}, u32[]{:S(2)}) copy-start(f32[1024]{0:T(1024)} %param.14) | copy-start | bytes 12292
  121.5 77.9 %collective-permute-start.1 = (bf16[16,1024]{1,0:T(8,128)(2,1)}, bf16[16,1024]{1,0:T(8,128)(2,1)}, u32[]{:S(2)}, u32[]{:S(2)}) collective-permute-start(bf16[16,1024]{1,0:T(8,128)(2,1)} %get-tuple-element.255), channel_id=1, source_target_pairs={{0,1},{1,2},{2,3},{3,4},{4,5},{5,6},{6,7},{7,0},{8,9},{9,10},{10,1... | collective-permute-start | bytes 98312 | tf_op jit(solution)/shard_map/ppermute | solution.py:25
  137.3 6.6 %copy-start.1 = (bf16[4,128,16,64]{1,3,2,0:T(8,128)(2,1)S(1)}, bf16[4,128,16,64]{1,3,2,0:T(8,128)(2,1)}, u32[]{:S(2)}) copy-start(bf16[4,128,16,64]{1,3,2,0:T(8,128)(2,1)} %copy.70) | copy-start | bytes 3145732
  147.2 1.4 copy-start.2
  147.2 1.4 copy-start.5
  147.2 1.5 copy-start.7
  198.2 48.4 %copy-start.9 = (f32[2,16,256]{2,1,0:T(8,128)S(1)}, f32[2,16,256]{2,1,0:T(8,128)}, u32[]{:S(2)}) copy-start(f32[2,16,256]{2,1,0:T(8,128)} %custom-call.3) | copy-start | bytes 98308
  199.4 6.9 %collective-permute-start.2 = (bf16[16,1024]{1,0:T(8,128)(2,1)}, bf16[16,1024]{1,0:T(8,128)(2,1)S(1)}, u32[]{:S(2)}, u32[]{:S(2)}) collective-permute-start(bf16[16,1024]{1,0:T(8,128)(2,1)} %collective-permute-done.1), channel_id=1, source_target_pairs={{0,1},{1,2},{2,3},{3,4},{4,5},{5,6},{6,7},{7,0},{8,9},{9,10},{10,1... | collective-permute-start | bytes 98312 | tf_op jit(solution)/shard_map/ppermute | solution.py:25
  206.2 6.6 %collective-permute-start.3 = (bf16[16,1024]{1,0:T(8,128)(2,1)S(1)}, bf16[16,1024]{1,0:T(8,128)(2,1)S(1)}, u32[]{:S(2)}, u32[]{:S(2)}) collective-permute-start(bf16[16,1024]{1,0:T(8,128)(2,1)S(1)} %collective-permute-done.2), channel_id=1, source_target_pairs={{0,1},{1,2},{2,3},{3,4},{4,5},{5,6},{6,7},{7,0},{8,9},{9,10},{10,1... | collective-permute-start | bytes 98312 | tf_op jit(solution)/shard_map/ppermute | solution.py:25
  212.9 6.6 %collective-permute-start.4 = (bf16[16,1024]{1,0:T(8,128)(2,1)S(1)}, bf16[16,1024]{1,0:T(8,128)(2,1)S(1)}, u32[]{:S(2)}, u32[]{:S(2)}) collective-permute-start(bf16[16,1024]{1,0:T(8,128)(2,1)S(1)} %collective-permute-done.3), channel_id=1, source_target_pairs={{0,1},{1,2},{2,3},{3,4},{4,5},{5,6},{6,7},{7,0},{8,9},{9,10},{10,1... | collective-permute-start | bytes 98312 | tf_op jit(solution)/shard_map/ppermute | solution.py:25
  219.5 6.8 %collective-permute-start.5 = (bf16[16,1024]{1,0:T(8,128)(2,1)S(1)}, bf16[16,1024]{1,0:T(8,128)(2,1)S(1)}, u32[]{:S(2)}, u32[]{:S(2)}) collective-permute-start(bf16[16,1024]{1,0:T(8,128)(2,1)S(1)} %collective-permute-done.4), channel_id=1, source_target_pairs={{0,1},{1,2},{2,3},{3,4},{4,5},{5,6},{6,7},{7,0},{8,9},{9,10},{10,1... | collective-permute-start | bytes 98312 | tf_op jit(solution)/shard_map/ppermute | solution.py:25
  226.3 6.6 %collective-permute-start.6 = (bf16[16,1024]{1,0:T(8,128)(2,1)S(1)}, bf16[16,1024]{1,0:T(8,128)(2,1)S(1)}, u32[]{:S(2)}, u32[]{:S(2)}) collective-permute-start(bf16[16,1024]{1,0:T(8,128)(2,1)S(1)} %collective-permute-done.5), channel_id=1, source_target_pairs={{0,1},{1,2},{2,3},{3,4},{4,5},{5,6},{6,7},{7,0},{8,9},{9,10},{10,1... | collective-permute-start | bytes 98312 | tf_op jit(solution)/shard_map/ppermute | solution.py:25
  232.9 6.6 %collective-permute-start.7 = (bf16[16,1024]{1,0:T(8,128)(2,1)S(1)}, bf16[16,1024]{1,0:T(8,128)(2,1)S(1)}, u32[]{:S(2)}, u32[]{:S(2)}) collective-permute-start(bf16[16,1024]{1,0:T(8,128)(2,1)S(1)} %collective-permute-done.6), channel_id=1, source_target_pairs={{0,1},{1,2},{2,3},{3,4},{4,5},{5,6},{6,7},{7,0},{8,9},{9,10},{10,1... | collective-permute-start | bytes 98312 | tf_op jit(solution)/shard_map/ppermute | solution.py:25
  247.4 2.9 %copy-start.3 = (f32[2,16,256,64]{2,3,1,0:T(8,128)S(1)}, f32[2,16,256,64]{2,3,1,0:T(8,128)}, u32[]{:S(2)}) copy-start(f32[2,16,256,64]{2,3,1,0:T(8,128)} %get-tuple-element.361) | copy-start | bytes 6291460 | tf_op jit(solution)/shard_map/while
  247.4 2.9 %copy-start.6 = (bf16[128,16,64]{0,2,1:T(8,128)(2,1)S(1)}, bf16[128,16,64]{0,2,1:T(8,128)(2,1)}, u32[]{:S(2)}) copy-start(bf16[128,16,64]{0,2,1:T(8,128)(2,1)} %get-tuple-element.380) | copy-start | bytes 786436 | tf_op jit(solution)/shard_map/while
  251.0 1.3 copy-start.4
  253.2 2.9 %copy-start.3 = (f32[2,16,256,64]{2,3,1,0:T(8,128)S(1)}, f32[2,16,256,64]{2,3,1,0:T(8,128)}, u32[]{:S(2)}) copy-start(f32[2,16,256,64]{2,3,1,0:T(8,128)} %get-tuple-element.361) | copy-start | bytes 6291460 | tf_op jit(solution)/shard_map/while
  253.2 2.9 %copy-start.6 = (bf16[128,16,64]{0,2,1:T(8,128)(2,1)S(1)}, bf16[128,16,64]{0,2,1:T(8,128)(2,1)}, u32[]{:S(2)}) copy-start(bf16[128,16,64]{0,2,1:T(8,128)(2,1)} %get-tuple-element.380) | copy-start | bytes 786436 | tf_op jit(solution)/shard_map/while
  256.8 1.3 copy-start.4
  260.0 1.4 copy-start.16
  261.4 2.9 copy-start.13
  261.4 2.9 copy-start.15
  264.3 19.4 %copy-start.14 = (bf16[512,1024]{1,0:T(8,128)(2,1)}, bf16[512,1024]{1,0:T(8,128)(2,1)S(1)}, u32[]{:S(2)}) copy-start(bf16[512,1024]{1,0:T(8,128)(2,1)S(1)} %fusion.53) | copy-start | bytes 3145732
  265.6 13.7 %all-to-all-start = ((bf16[8,32,1024]{2,1,0:T(8,128)(2,1)}), bf16[8,32,1024]{2,1,0:T(8,128)(2,1)S(1)}, u32[]{:S(2)}, u32[]{:S(2)}) async-start(bf16[8,32,1024]{2,1,0:T(8,128)(2,1)} %bitcast.28), calls=%async_computation | async-start | bytes 1048576 | tf_op jit(solution)/shard_map/all_to_all | solution.py:244
Sparse Core Ops, SparseCore 0:
  10.0 102.5 all-gather.4
  114.7 50.4 all-gather.6
  166.8 32.5 all-gather.8
